TPU v7x, 128 devices: a whole 4x4x4 slice. The times are simulated.
128 devices in a mesh: dp: 16 (over x, y), tensor: 8 (over z, core).
Axes of the slice: x: 4, y: 4, z: 4, core: 2. Of those that a mesh axis runs over, the one named last changes fastest.
Arguments:
- kv_part: bfloat16 [8, 4096, 12288], P('tensor', 'dp'), may hold values from -2 to 2
- queries: bfloat16 [8192, 6144], P('dp', 'tensor'), may hold values from -6 to 6
- w_out: bfloat16 [6144, 8192], P('tensor'), may hold values from -0.078125 to 0.078125
- d_out: bfloat16 [8192, 8192], P('dp', 'tensor'), may hold values from -48 to 48
- nbr_owner: int32 [128, 2], replicated, may hold values from 0 to 15, as said below
- nbr_slot: int32 [128, 2], replicated, may hold values from 0 to 1, as said below
Outputs:
- mixed: bfloat16 [8192, 8192], P('dp', 'tensor')
- d_kv: bfloat16 [4096, 12288], P('dp', 'tensor')
Inputs may be any that keep to these rules, and one draw needn't show every extreme that they name: `nbr_owner`: the two neighbours of one span have different owners. `nbr_slot`: all neighbours that the spans of one dp index r (spans r * 8 to (r + 1) * 8 - 1) take from one owner have the same slot.
All inputs are finite; a program needn't handle non-finite values.
Results may differ from a plain program's by a relative error of at most 0.025.
Values may be sent and summed in bfloat16 or wider, within the bound.
A program may use at most 192 MiB of HBM per device.

v0:
```python
import jax
import jax.numpy as jnp
from jax import lax
from jax.sharding import PartitionSpec as P

HD = 128
SPAN = 64
NBR_LEN = 128
NB_DEV = 2


def local(kv_part, queries, w_out, d_out, nbr_owner, nbr_slot):
    dp_count = lax.axis_size("dp")
    reader = lax.axis_index("dp")
    head_width = w_out.shape[0]
    heads_here = head_width // HD
    share_width = 2 * head_width
    span_count = queries.shape[0] // SPAN
    read_count = 2 * span_count
    block_width = NBR_LEN * share_width
    local_partial = kv_part[0]
    summed = lax.psum(local_partial, "tensor").astype(jnp.float32)
    shares = lax.dynamic_slice_in_dim(
        summed, lax.axis_index("tensor") * share_width, share_width, 1
    ).astype(jnp.bfloat16)
    share_blocks = shares.reshape(NB_DEV, block_width)
    owner_ids = jnp.arange(dp_count, dtype=jnp.int32)
    slot_ids = jnp.arange(NB_DEV, dtype=jnp.int32)
    owner_hits = nbr_owner[:, :, None] == owner_ids[None, None, :]
    per_reader = owner_hits.reshape(dp_count, read_count, dp_count)
    reads_from = jnp.any(per_reader, axis=1)
    slot_from = jnp.max(jnp.where(per_reader, nbr_slot.reshape(dp_count, read_count, 1), 0), axis=1)
    my_owner = lax.dynamic_slice_in_dim(nbr_owner, reader * span_count, span_count, 0).reshape(
        read_count
    )
    my_slot = lax.dynamic_slice_in_dim(nbr_slot, reader * span_count, span_count, 0).reshape(
        read_count
    )
    read_table = (my_owner[:, None] == owner_ids[None, :]).astype(jnp.bfloat16)
    serving = lax.dynamic_index_in_dim(reads_from, reader, 1, False)
    serving_slot = lax.dynamic_index_in_dim(slot_from, reader, 1, False)
    owner_select = ((serving_slot[:, None] == slot_ids[None, :]) & serving[:, None]).astype(
        jnp.bfloat16
    )
    everyone = lax.all_gather(share_blocks, "dp", axis=0, tiled=True)
    wanted = (my_owner * NB_DEV + my_slot)[:, None] == jnp.arange(
        dp_count * NB_DEV, dtype=jnp.int32
    )[None, :]
    neighbours = jnp.dot(
        wanted.astype(jnp.bfloat16), everyone, preferred_element_type=jnp.float32
    ).astype(jnp.bfloat16)
    layout = neighbours.reshape(span_count, 2 * NBR_LEN, heads_here, 2, HD)
    keys = layout[:, :, :, 0]
    values = layout[:, :, :, 1]
    query_view = queries.reshape(span_count, SPAN, heads_here, HD)
    factor = HD ** (-0.5)
    scores = (
        jnp.einsum("cqhd,ckhd->chqk", query_view, keys, preferred_element_type=jnp.float32) * factor
    )
    highest = jnp.max(scores, axis=-1, keepdims=True)
    expo = jnp.exp(scores - highest)
    probs = expo / jnp.sum(expo, axis=-1, keepdims=True)
    probs_low = probs.astype(jnp.bfloat16)
    attended = jnp.einsum("chqk,ckhd->cqhd", probs_low, values, preferred_element_type=jnp.float32)
    attended = attended.astype(jnp.bfloat16).reshape(span_count * SPAN, head_width)
    partial_out = jnp.dot(attended, w_out, preferred_element_type=jnp.float32)
    mixed = lax.psum_scatter(
        partial_out.astype(jnp.bfloat16), "tensor", scatter_dimension=1, tiled=True
    )
    grad_attended = lax.dot_general(
        lax.all_gather(d_out, "tensor", axis=1, tiled=True),
        w_out,
        (((1,), (1,)), ((), ())),
        preferred_element_type=jnp.float32,
    ).astype(jnp.bfloat16)
    grad_view = grad_attended.reshape(span_count, SPAN, heads_here, HD)
    grad_values = jnp.einsum(
        "chqk,cqhd->ckhd", probs_low, grad_view, preferred_element_type=jnp.float32
    )
    grad_probs = jnp.einsum(
        "cqhd,ckhd->chqk", grad_view, values, preferred_element_type=jnp.float32
    )
    grad_scores = probs * (grad_probs - jnp.sum(probs * grad_probs, axis=-1, keepdims=True))
    grad_scores = grad_scores.astype(jnp.bfloat16)
    grad_keys = (
        jnp.einsum("chqk,cqhd->ckhd", grad_scores, query_view, preferred_element_type=jnp.float32)
        * factor
    )
    grad_blocks = jnp.stack([grad_keys, grad_values], axis=3).reshape(read_count, block_width)
    per_owner = lax.dot_general(
        read_table.astype(jnp.float32),
        grad_blocks,
        (((0,), (0,)), ((), ())),
        precision=lax.Precision.HIGHEST,
        preferred_element_type=jnp.float32,
    ).astype(jnp.bfloat16)
    returned = lax.all_to_all(per_owner, "dp", split_axis=0, concat_axis=0, tiled=True)
    owner_grad = lax.dot_general(
        owner_select, returned, (((0,), (0,)), ((), ())), preferred_element_type=jnp.float32
    )
    d_kv = owner_grad.astype(jnp.bfloat16).reshape(NB_DEV * NBR_LEN, share_width)
    return (mixed, d_kv)


def solution(mesh):
    placed = (
        P("tensor", "dp", None),
        P("dp", "tensor"),
        P("tensor", None),
        P("dp", "tensor"),
        P(),
        P(),
    )
    return jax.shard_map(
        local,
        mesh=mesh,
        in_specs=placed,
        out_specs=(P("dp", "tensor"), P("dp", "tensor")),
        check_vma=False,
    )
```

profile of v0, /device:TPU:28, one launch (start us, length us, event | category | flops | bytes accessed | tf_op | source)
XLA Modules:
  0.0 541.4 jit_solution(5792027820581872935)
XLA Ops:
  7.2 0.7 all-reduce.2.cloned.1.call-update
  8.0 89.0 %all-reduce.2.cloned.1.call-done = bf16[256,12288]{1,0:T(8,128)(2,1)} async-done(((bf16[256,12288]{1,0:T(8,128)(2,1)}), bf16[256,12288]{1,0:T(8,128)(2,1)}) %all-reduce.2.cloned.1.call-update) | async-done | bytes 6291472 | tf_op jit(solution)/shard_map/psum | solution.py:22
  97.0 1.2 convert_convert_fusion
  98.2 1.5 reshape.62
  99.7 0.7 all-gather.4.cloned.1.call-update
  100.9 1.9 reshape.57
  102.8 85.0 %all-gather.6.cloned.1.call-done = bf16[16,2,196608]{2,1,0:T(2,128)(2,1)} async-done(((bf16[1,2,196608]{2,1,0:T(2,128)(2,1)}), bf16[16,2,196608]{2,1,0:T(2,128)(2,1)}) %all-gather.6.cloned.1.call-update) | async-done | bytes 12582928 | tf_op jit(solution)/shard_map/all_gather | solution.py:45
  187.7 11.3 %reshape.63 = bf16[32,196608]{1,0:T(8,128)(2,1)} reshape(bf16[16,2,196608]{2,1,0:T(2,128)(2,1)} %all-gather.6.cloned.1.call-done) | data formatting | bytes 25165824
  199.0 10.4 %convolution_convert_fusion.1 = bf16[16,196608]{1,0:T(8,128)(2,1)} fusion(bf16[32,196608]{1,0:T(8,128)(2,1)} %reshape.63, s32[16]{0:T(128)S(1)} %multiply_add_fusion), kind=kOutput, calls=%fused_computation.2 | convolution fusion | flops 204472832 | bytes 18874432 | tf_op jit(solution)/shard_map/dot_general | solution.py:49
  209.4 9.9 %reshape.56 = bf16[8,256,6,2,128]{4,3,2,1,0:T(2,128)(2,1)} reshape(bf16[16,196608]{1,0:T(8,128)(2,1)} %convolution_convert_fusion.1) | data formatting | bytes 12582912 | tf_op jit(solution)/shard_map/reshape | solution.py:52
  219.3 13.7 %fusion.42 = (bf16[8,256,6,1,128]{4,3,2,1,0:T(2,128)(2,1)S(1)}, bf16[8,256,6,1,128]{4,3,2,1,0:T(2,128)(2,1)}) fusion(bf16[8,256,6,2,128]{4,3,2,1,0:T(2,128)(2,1)} %reshape.56), kind=kLoop, calls=%fused_computation.54 | loop fusion | bytes 12582912 | tf_op jit(solution)/shard_map/slice | solution.py:53
  233.0 1.2 fusion.4
  234.2 2.3 fusion.43
  236.5 9.2 %fusion.12 = bf16[8,64,6,128]{3,1,2,0:T(8,128)(2,1)} fusion(bf16[8,256,6,1,128]{4,3,2,1,0:T(2,128)(2,1)} %get-tuple-element.3, f32[8,6,64]{2,1,0:T(8,128)S(1)} %get-tuple-element.4, f32[8,6,256,64]{2,3,1,0:T(8,128)S(1)} %fusion.4), kind=kOutput, calls=%fused_computation.27 | convolution fusion | flops 205655296 | bytes 7090176 | tf_op jit(solution)/shard_map/chqk,ckhd->cqhd/dot_general | solution.py:64
  245.7 1.7 copy.77
  247.4 13.4 %convolution_convert_fusion.3 = bf16[512,8192]{1,0:T(8,128)(2,1)} fusion(bf16[768,8192]{1,0:T(8,128)(2,1)} %param.8, bf16[64,8,6,128]{3,2,1,0:T(8,128)(2,1)S(1)} %bitcast.71), kind=kOutput, calls=%fused_computation.6 | convolution fusion | flops 6446645248 | bytes 21757952 | tf_op jit(solution)/shard_map/dot_general | solution.py:66
  260.9 13.5 %convolution_convert_fusion.5 = bf16[512,768]{1,0:T(8,128)(2,1)} fusion(bf16[512,8192]{1,0:T(8,128)(2,1)} %all-gather.4.cloned.1.call-done, bf16[768,8192]{1,0:T(8,128)(2,1)} %param.8), kind=kOutput, calls=%fused_computation.26 | convolution fusion | flops 6442844160 | bytes 21757952 | tf_op jit(solution)/shard_map/dot_general | solution.py:70
  274.4 2.9 reshape.59
  277.3 10.3 %convolution_bitcast_fusion = f32[8,256,6,1,128]{4,1,2,0,3:T(8,128)} fusion(bf16[8,64,6,128]{3,2,1,0:T(8,128)(2,1)} %reshape.59, f32[8,6,64]{2,1,0:T(8,128)S(1)} %get-tuple-element.4, f32[8,6,256,64]{2,3,1,0:T(8,128)S(1)} %fusion.4), kind=kOutput, calls=%fused_computation.20 | convolution fusion | flops 205262080 | bytes 10235904 | tf_op jit(solution)/shard_map/chqk,cqhd->ckhd/dot_general | solution.py:77
  287.6 7.2 %multiply_reduce_fusion = (f32[8,6,64]{2,1,0:T(8,128)S(1)}, f32[8,6,64,256]{3,2,1,0:T(8,128)}) fusion(f32[8,6,64,256]{3,2,1,0:T(8,128)} %get-tuple-element.5, f32[8,6,64]{2,1,0:T(8,128)S(1)} %get-tuple-element.4, bf16[8,256,6,1,128]{4,3,2,1,0:T(2,128)(2,1)} %get-tuple-element.3, bf16[8,64,6,128]{3,2,1,0:T(8,128)(2,1)} %reshape.59), kind=kOutput, calls=%fused_computation.18 | convolution fusion | flops 203682816 | bytes 10248192 | tf_op jit(solution)/shard_map/cqhd,ckhd->chqk/dot_general | solution.py:80
  294.8 11.7 %multiply_bitcast_fusion = f32[8,256,6,1,128]{4,1,2,0,3:T(8,128)} fusion(f32[8,6,64,256]{3,2,1,0:T(8,128)} %get-tuple-element.7, f32[8,6,64]{2,1,0:T(8,128)S(1)} %get-tuple-element.6, bf16[8,64,6,128]{3,2,1,0:T(8,128)(2,1)} %reshape.57, f32[8,6,64]{2,1,0:T(8,128)S(1)} %get-tuple-element.4, f32[8,6,256,64]{2,3,1,0:T(8,128)S(1)} %fusion.4), kind=kOutput, calls=%fused_computation.9 | convolution fusion | flops 208407808 | bytes 13393920 | tf_op jit(solution)/shard_map/chqk,cqhd->ckhd/dot_general | solution.py:86
  306.5 10.9 %pad_maximum_fusion = f32[8,256,6,2,128]{4,1,2,0,3:T(8,128)} fusion(f32[8,256,6,1,128]{4,1,2,0,3:T(8,128)} %convolution_bitcast_fusion, f32[8,256,6,1,128]{4,1,2,0,3:T(8,128)} %multiply_bitcast_fusion), kind=kLoop, calls=%fused_computation.5 | loop fusion | flops 3145728 | bytes 25165824 | tf_op jit(solution)/shard_map/stack | solution.py:89
  317.4 22.2 %copy.84 = f32[8,256,6,2,128]{4,3,2,1,0:T(2,128)} copy(f32[8,256,6,2,128]{4,1,2,0,3:T(8,128)} %pad_maximum_fusion) | data formatting | bytes 25165824 | tf_op jit(solution)/shard_map/stack | solution.py:89
  339.6 21.3 %reshape.60 = f32[16,196608]{1,0:T(8,128)} reshape(f32[8,256,6,2,128]{4,3,2,1,0:T(2,128)} %copy.84) | data formatting | bytes 25165824 | tf_op jit(solution)/shard_map/reshape | solution.py:89
  360.9 10.9 %fusion.1 = bf16[16,1,196608]{2,0,1:T(8,128)(2,1)} fusion(f32[16,196608]{1,0:T(8,128)} %reshape.60, s32[16]{0:T(128)S(1)} %reshape.53), kind=kOutput, calls=%fused_computation.3 | convolution fusion | flops 607125760 | bytes 18874432 | tf_op jit(solution)/shard_map/dot_general | solution.py:90
  372.3 8.8 %reduce.4 = bf16[16,196608]{1,0:T(8,128)(2,1)} reduce(bf16[16,1,196608]{2,0,1:T(8,128)(2,1)} %fusion.1, bf16[]{:T(256)} %broadcast.20), dimensions={1}, to_apply=%copy.85.reduce_sub_computation | reduce | bytes 12582914 | tf_op jit(solution)/shard_map/all_to_all | solution.py:97
  381.2 9.3 %reshape.67 = bf16[16,2,98304]{2,1,0:T(2,128)(2,1)} reshape(bf16[16,196608]{1,0:T(8,128)(2,1)} %reduce.4) | data formatting | bytes 12582912
  390.5 7.2 %all-to-all-start = ((bf16[16,2,98304]{2,1,0:T(2,128)(2,1)}), bf16[16,2,98304]{2,1,0:T(2,128)(2,1)}, u32[]{:S(2)}, u32[]{:S(2)}) async-start(bf16[16,2,98304]{2,1,0:T(2,128)(2,1)} %reshape.67), calls=%async_computation.1 | async-start | bytes 12582912 | tf_op jit(solution)/shard_map/all_to_all | solution.py:97
  398.8 107.1 %all-to-all-done = bf16[16,2,98304]{2,1,0:T(2,128)(2,1)} async-done(((bf16[16,2,98304]{2,1,0:T(2,128)(2,1)}), bf16[16,2,98304]{2,1,0:T(2,128)(2,1)}, u32[]{:S(2)}, u32[]{:S(2)}) %all-to-all-start) | async-done | bytes 6291488 | tf_op jit(solution)/shard_map/all_to_all | solution.py:97
  505.9 14.3 %reshape.68 = bf16[16,1,196608]{2,1,0:T(2,128)(2,1)} reshape(bf16[16,2,98304]{2,1,0:T(2,128)(2,1)} %all-to-all-done) | data formatting | bytes 12582912
  520.2 12.8 %convolution_convert_fusion.2 = bf16[2,196608]{1,0:T(2,128)(2,1)S(1)} fusion(bf16[16,1,196608]{2,1,0:T(2,128)(2,1)} %reshape.68, s32[16]{0:T(128)S(1)} %dynamic-slice_reduce_fusion, pred[16]{0:T(512)(128)(4,1)S(1)} %dynamic-slice_reduce_fusion.1), kind=kOutput, calls=%fused_computation.4 | convolution fusion | flops 12976192 | bytes 7077968 | tf_op jit(solution)/shard_map/dot_general | solution.py:98
  533.1 1.6 reshape.61
  (31 shorter events, 2.2 us)
Async XLA Ops:
  7.2 89.8 %all-reduce.2.cloned.1.call-start = ((), (), s32[]{:S(2)}) async-start(), calls=%async_computation.2 | async-start | bytes 12582912 | tf_op jit(solution)/shard_map/psum | solution.py:22
  7.9 92.6 %copy-start.2 = (s32[128,2]{0,1:T(2,128)S(1)}, s32[128,2]{0,1:T(2,128)}, u32[]{:S(2)}) copy-start(s32[128,2]{0,1:T(2,128)} %param.11) | copy-start | bytes 3076
  7.9 92.6 %copy-start.3 = (s32[128,2]{0,1:T(2,128)S(1)}, s32[128,2]{0,1:T(2,128)}, u32[]{:S(2)}) copy-start(s32[128,2]{0,1:T(2,128)} %param.10) | copy-start | bytes 3076
  7.9 93.0 %copy-start.1 = (bf16[512,768]{1,0:T(8,128)(2,1)S(1)}, bf16[512,768]{1,0:T(8,128)(2,1)}, u32[]{:S(2)}) copy-start(bf16[512,768]{1,0:T(8,128)(2,1)} %param.7) | copy-start | bytes 2359300
  7.9 179.8 %all-gather.6.cloned.1.call-start = ((), (), s32[]{:S(2)}) async-start(), calls=%async_computation.5 | async-start | bytes 13369344 | tf_op jit(solution)/shard_map/all_gather | solution.py:45
  99.7 161.2 %all-gather.4.cloned.1.call-start = ((), (), s32[]{:S(2)}) async-start(), calls=%async_computation.4 | async-start | bytes 9437184 | tf_op jit(solution)/shard_map/all_gather | solution.py:71
  100.4 434.3 %reduce-scatter.2.cloned.1.call-start = ((), (), s32[]{:S(2)}) async-start(), calls=%async_computation.3 | async-start | bytes 9437184 | tf_op jit(solution)/shard_map/reduce_scatter | solution.py:67
  219.3 13.7 %copy-start = (bf16[8,64,6,128]{3,2,1,0:T(8,128)(2,1)S(1)}, bf16[8,64,6,128]{3,2,1,0:T(8,128)(2,1)}, u32[]{:S(2)}) copy-start(bf16[8,64,6,128]{3,2,1,0:T(8,128)(2,1)} %reshape.57) | copy-start | bytes 2359300
  390.5 115.4 %all-to-all-start = ((bf16[16,2,98304]{2,1,0:T(2,128)(2,1)}), bf16[16,2,98304]{2,1,0:T(2,128)(2,1)}, u32[]{:S(2)}, u32[]{:S(2)}) async-start(bf16[16,2,98304]{2,1,0:T(2,128)(2,1)} %reshape.67), calls=%async_computation.1 | async-start | bytes 12582912 | tf_op jit(solution)/shard_map/all_to_all | solution.py:97
Sparse Core Ops, SparseCore 0:
  10.4 86.5 all-reduce.1
  99.8 87.8 all-gather.5
  189.4 51.1 all-gather.3
  261.0 53.9 reduce-scatter.1
where the time goes:
time: 549 us; the launch traced here: 541 us
  waiting for transfers between devices  283 us (52%)
  local copies, waits for them, and re-layouts  113 us (21%)
  matrix products  101 us (18%)
  other arithmetic  23.6 us (4%)
  between operations  14.1 us (3%)
  starting transfers between devices  7.38 us (1%)
    all_to_all x1, waiting for transfers between devices, local(): lax.all_to_all(per_owner, 'dp', split_axis=0, concat_axis=0, tiled=True)  107 us
    psum x1, waiting for transfers between devices, local(): summed = lax.psum(local_partial, 'tensor').astype(jnp.float32)  89 us
    all_gather x1, waiting for transfers between devices, local(): everyone = lax.all_gather(share_blocks, 'dp', axis=0, tiled=True)  85 us
    unnamed x14, local copies, waits for them, and re-layouts  36.7 us
    another operation x1, local copies, waits for them, and re-layouts, local(): jnp.stack([grad_keys, grad_values], axis=3).reshape(read_count, block_width)  22.2 us
    reshape x1, local copies, waits for them, and re-layouts, local(): jnp.stack([grad_keys, grad_values], axis=3).reshape(read_count, block_width)  21.3 us
    slice x1, local copies, waits for them, and re-layouts, local(): keys = layout[:, :, :, 0]  13.7 us
    dot_general x1, matrix products, local(): lax.dot_general(lax.all_gather(d_out, 'tensor', axis=1, tiled=True), w_ou...  13.5 us
  transfers between devices with their start and end apart: 5, of which 3 were waited for; matrix products, arithmetic and copies ran while one was open for 43% of the time, Pallas kernels for 0%

commit v1 on v0

--- a/solution.py
+++ b/solution.py
@@ -42,7 +42,9 @@
     owner_select = ((serving_slot[:, None] == slot_ids[None, :]) & serving[:, None]).astype(
         jnp.bfloat16
     )
-    everyone = lax.all_gather(share_blocks, "dp", axis=0, tiled=True)
+    everyone = jnp.concatenate(
+        lax.all_to_all(jnp.stack([share_blocks] * lax.axis_size("dp")), "dp", 0, 0), axis=0
+    )
     wanted = (my_owner * NB_DEV + my_slot)[:, None] == jnp.arange(
         dp_count * NB_DEV, dtype=jnp.int32
     )[None, :]

time: 549 us -> 716 us (1.30)
  the two profiles are of different devices: /device:TPU:28 before, /device:TPU:60 now
where the time goes in v1:
time: 716 us; the launch traced here: 708 us
  waiting for transfers between devices  433 us (60%)
  local copies, waits for them, and re-layouts  123 us (17%)
  matrix products  99.3 us (14%)
  other arithmetic  23.7 us (3%)
  starting transfers between devices  14.4 us (2%)
  between operations  14 us (2%)
    all_to_all x1, waiting for transfers between devices, local(): lax.all_to_all(jnp.stack([share_blocks] * lax.axis_size('dp')), 'dp', 0, 0)  236 us
    all_to_all x1, waiting for transfers between devices, local(): lax.all_to_all(per_owner, 'dp', split_axis=0, concat_axis=0, tiled=True)  109 us
    psum x1, waiting for transfers between devices, local(): summed = lax.psum(local_partial, 'tensor').astype(jnp.float32)  86.3 us
    unnamed x12, local copies, waits for them, and re-layouts  23.9 us
    another operation x1, local copies, waits for them, and re-layouts, local(): jnp.stack([grad_keys, grad_values], axis=3).reshape(read_count, block_width)  22.2 us
    reshape x1, local copies, waits for them, and re-layouts, local(): jnp.stack([grad_keys, grad_values], axis=3).reshape(read_count, block_width)  21.3 us
  transfers between devices with their start and end apart: 5, of which 3 were waited for; matrix products, arithmetic and copies ran while one was open for 33% of the time, Pallas kernels for 0%

profile of v1, /device:TPU:60, one launch (start us, length us, event | category | flops | bytes accessed | tf_op | source)
XLA Modules:
  0.0 707.8 jit_solution(16700150028126672610)
XLA Ops:
  7.9 86.3 %all-reduce.2.cloned.1.call-done = bf16[256,12288]{1,0:T(8,128)(2,1)} async-done(((bf16[256,12288]{1,0:T(8,128)(2,1)}), bf16[256,12288]{1,0:T(8,128)(2,1)}) %all-reduce.2.cloned.1.call-update) | async-done | bytes 6291472 | tf_op jit(solution)/shard_map/psum | solution.py:22
  94.2 1.2 convert_convert_fusion
  95.9 10.9 %stack.12 = bf16[16,2,196608]{2,1,0:T(2,128)(2,1)} broadcast(bf16[2,196608]{1,0:T(2,128)(2,1)S(1)} %stack_reshape.2), dimensions={1,2} | broadcast | bytes 13369344 | tf_op jit(solution)/shard_map/stack | solution.py:46
  106.8 7.3 %all-to-all-start = ((bf16[16,2,196608]{2,1,0:T(2,128)(2,1)}), bf16[16,2,196608]{2,1,0:T(2,128)(2,1)}, u32[]{:S(2)}, u32[]{:S(2)}) async-start(bf16[16,2,196608]{2,1,0:T(2,128)(2,1)} %stack.12), calls=%async_computation | async-start | bytes 25165824 | tf_op jit(solution)/shard_map/all_to_all | solution.py:46
  114.2 0.7 all-gather.2.cloned.1.call-update
  115.4 1.9 reshape.59
  117.3 236.4 %all-to-all-done = bf16[16,2,196608]{2,1,0:T(2,128)(2,1)} async-done(((bf16[16,2,196608]{2,1,0:T(2,128)(2,1)}), bf16[16,2,196608]{2,1,0:T(2,128)(2,1)}, u32[]{:S(2)}, u32[]{:S(2)}) %all-to-all-start) | async-done | bytes 12582944 | tf_op jit(solution)/shard_map/all_to_all | solution.py:46
  353.6 11.3 %reshape.57 = bf16[32,196608]{1,0:T(8,128)(2,1)} reshape(bf16[16,2,196608]{2,1,0:T(2,128)(2,1)} %all-to-all-done) | data formatting | bytes 25165824 | tf_op jit(solution)/shard_map/reshape | solution.py:45
  364.9 9.1 %convolution_convert_fusion.1 = bf16[16,196608]{1,0:T(8,128)(2,1)} fusion(bf16[32,196608]{1,0:T(8,128)(2,1)} %reshape.57, s32[16]{0:T(128)S(1)} %multiply_add_fusion), kind=kOutput, calls=%fused_computation.2 | convolution fusion | flops 204472832 | bytes 18874432 | tf_op jit(solution)/shard_map/dot_general | solution.py:51
  374.1 9.8 %reshape.58 = bf16[8,256,6,2,128]{4,3,2,1,0:T(2,128)(2,1)} reshape(bf16[16,196608]{1,0:T(8,128)(2,1)} %convolution_convert_fusion.1) | data formatting | bytes 12582912 | tf_op jit(solution)/shard_map/reshape | solution.py:54
  383.9 13.7 %fusion.42 = (bf16[8,256,6,1,128]{4,3,2,1,0:T(2,128)(2,1)S(1)}, bf16[8,256,6,1,128]{4,3,2,1,0:T(2,128)(2,1)}) fusion(bf16[8,256,6,2,128]{4,3,2,1,0:T(2,128)(2,1)} %reshape.58), kind=kLoop, calls=%fused_computation.54 | loop fusion | bytes 12582912 | tf_op jit(solution)/shard_map/slice | solution.py:55
  397.6 1.2 fusion.4
  398.8 2.3 fusion.43
  401.1 9.1 %fusion.12 = bf16[8,64,6,128]{3,1,2,0:T(8,128)(2,1)} fusion(bf16[8,256,6,1,128]{4,3,2,1,0:T(2,128)(2,1)} %get-tuple-element.3, f32[8,6,64]{2,1,0:T(8,128)S(1)} %get-tuple-element.4, f32[8,6,256,64]{2,3,1,0:T(8,128)S(1)} %fusion.4), kind=kOutput, calls=%fused_computation.27 | convolution fusion | flops 205655296 | bytes 7090176 | tf_op jit(solution)/shard_map/chqk,ckhd->cqhd/dot_general | solution.py:66
  410.3 1.7 copy.77
  411.9 13.4 %convolution_convert_fusion.3 = bf16[512,8192]{1,0:T(8,128)(2,1)} fusion(bf16[768,8192]{1,0:T(8,128)(2,1)} %param.8, bf16[64,8,6,128]{3,2,1,0:T(8,128)(2,1)S(1)} %bitcast.71), kind=kOutput, calls=%fused_computation.6 | convolution fusion | flops 6446645248 | bytes 21757952 | tf_op jit(solution)/shard_map/dot_general | solution.py:68
  425.4 13.5 %convolution_convert_fusion.5 = bf16[512,768]{1,0:T(8,128)(2,1)} fusion(bf16[512,8192]{1,0:T(8,128)(2,1)} %all-gather.2.cloned.1.call-done, bf16[768,8192]{1,0:T(8,128)(2,1)} %param.8), kind=kOutput, calls=%fused_computation.26 | convolution fusion | flops 6442844160 | bytes 21757952 | tf_op jit(solution)/shard_map/dot_general | solution.py:72
  438.9 2.9 reshape.61
  441.9 10.3 %convolution_bitcast_fusion = f32[8,256,6,1,128]{4,1,2,0,3:T(8,128)} fusion(bf16[8,64,6,128]{3,2,1,0:T(8,128)(2,1)} %reshape.61, f32[8,6,64]{2,1,0:T(8,128)S(1)} %get-tuple-element.4, f32[8,6,256,64]{2,3,1,0:T(8,128)S(1)} %fusion.4), kind=kOutput, calls=%fused_computation.20 | convolution fusion | flops 205262080 | bytes 10235904 | tf_op jit(solution)/shard_map/chqk,cqhd->ckhd/dot_general | solution.py:79
  452.1 7.2 %multiply_reduce_fusion = (f32[8,6,64]{2,1,0:T(8,128)S(1)}, f32[8,6,64,256]{3,2,1,0:T(8,128)}) fusion(f32[8,6,64,256]{3,2,1,0:T(8,128)} %get-tuple-element.5, f32[8,6,64]{2,1,0:T(8,128)S(1)} %get-tuple-element.4, bf16[8,256,6,1,128]{4,3,2,1,0:T(2,128)(2,1)} %get-tuple-element.3, bf16[8,64,6,128]{3,2,1,0:T(8,128)(2,1)} %reshape.61), kind=kOutput, calls=%fused_computation.18 | convolution fusion | flops 203682816 | bytes 10248192 | tf_op jit(solution)/shard_map/cqhd,ckhd->chqk/dot_general | solution.py:82
  459.4 11.7 %multiply_bitcast_fusion = f32[8,256,6,1,128]{4,1,2,0,3:T(8,128)} fusion(f32[8,6,64,256]{3,2,1,0:T(8,128)} %get-tuple-element.7, f32[8,6,64]{2,1,0:T(8,128)S(1)} %get-tuple-element.6, bf16[8,64,6,128]{3,2,1,0:T(8,128)(2,1)} %reshape.59, f32[8,6,64]{2,1,0:T(8,128)S(1)} %get-tuple-element.4, f32[8,6,256,64]{2,3,1,0:T(8,128)S(1)} %fusion.4), kind=kOutput, calls=%fused_computation.9 | convolution fusion | flops 208407808 | bytes 13393920 | tf_op jit(solution)/shard_map/chqk,cqhd->ckhd/dot_general | solution.py:88
  471.1 11.0 %pad_maximum_fusion = f32[8,256,6,2,128]{4,1,2,0,3:T(8,128)} fusion(f32[8,256,6,1,128]{4,1,2,0,3:T(8,128)} %convolution_bitcast_fusion, f32[8,256,6,1,128]{4,1,2,0,3:T(8,128)} %multiply_bitcast_fusion), kind=kLoop, calls=%fused_computation.5 | loop fusion | flops 3145728 | bytes 25165824 | tf_op jit(solution)/shard_map/stack | solution.py:91
  482.1 22.2 %copy.84 = f32[8,256,6,2,128]{4,3,2,1,0:T(2,128)} copy(f32[8,256,6,2,128]{4,1,2,0,3:T(8,128)} %pad_maximum_fusion) | data formatting | bytes 25165824 | tf_op jit(solution)/shard_map/stack | solution.py:91
  504.2 21.3 %reshape.62 = f32[16,196608]{1,0:T(8,128)} reshape(f32[8,256,6,2,128]{4,3,2,1,0:T(2,128)} %copy.84) | data formatting | bytes 25165824 | tf_op jit(solution)/shard_map/reshape | solution.py:91
  525.5 10.9 %fusion.1 = bf16[16,1,196608]{2,0,1:T(8,128)(2,1)} fusion(f32[16,196608]{1,0:T(8,128)} %reshape.62, s32[16]{0:T(128)S(1)} %reshape.55), kind=kOutput, calls=%fused_computation.3 | convolution fusion | flops 607125760 | bytes 18874432 | tf_op jit(solution)/shard_map/dot_general | solution.py:92
  537.0 8.8 %reduce.4 = bf16[16,196608]{1,0:T(8,128)(2,1)} reduce(bf16[16,1,196608]{2,0,1:T(8,128)(2,1)} %fusion.1, bf16[]{:T(256)} %broadcast.21), dimensions={1}, to_apply=%copy.85.reduce_sub_computation | reduce | bytes 12582914 | tf_op jit(solution)/shard_map/all_to_all | solution.py:99
  545.8 9.3 %reshape.66 = bf16[16,2,98304]{2,1,0:T(2,128)(2,1)} reshape(bf16[16,196608]{1,0:T(8,128)(2,1)} %reduce.4) | data formatting | bytes 12582912
  555.2 6.9 all-to-all-start.1
  563.1 109.2 %all-to-all-done.1 = bf16[16,2,98304]{2,1,0:T(2,128)(2,1)} async-done(((bf16[16,2,98304]{2,1,0:T(2,128)(2,1)}), bf16[16,2,98304]{2,1,0:T(2,128)(2,1)}, u32[]{:S(2)}, u32[]{:S(2)}) %all-to-all-start.1) | async-done | bytes 6291488 | tf_op jit(solution)/shard_map/all_to_all | solution.py:99
  672.3 14.3 %reshape.67 = bf16[16,1,196608]{2,1,0:T(2,128)(2,1)} reshape(bf16[16,2,98304]{2,1,0:T(2,128)(2,1)} %all-to-all-done.1) | data formatting | bytes 12582912
  686.6 12.8 %convolution_convert_fusion.2 = bf16[2,196608]{1,0:T(2,128)(2,1)S(1)} fusion(bf16[16,1,196608]{2,1,0:T(2,128)(2,1)} %reshape.67, s32[16]{0:T(128)S(1)} %dynamic-slice_reduce_fusion, pred[16]{0:T(512)(128)(4,1)S(1)} %dynamic-slice_reduce_fusion.1), kind=kOutput, calls=%fused_computation.4 | convolution fusion | flops 12976192 | bytes 7077968 | tf_op jit(solution)/shard_map/dot_general | solution.py:100
  699.5 1.6 reshape.63
  (31 shorter events, 3.4 us)
Async XLA Ops:
  7.2 87.0 %all-reduce.2.cloned.1.call-start = ((), (), s32[]{:S(2)}) async-start(), calls=%async_computation.3 | async-start | bytes 12582912 | tf_op jit(solution)/shard_map/psum | solution.py:22
  106.8 8.2 %copy-start.2 = (s32[128,2]{0,1:T(2,128)S(1)}, s32[128,2]{0,1:T(2,128)}, u32[]{:S(2)}) copy-start(s32[128,2]{0,1:T(2,128)} %param.11) | copy-start | bytes 3076
  106.8 8.2 %copy-start.3 = (s32[128,2]{0,1:T(2,128)S(1)}, s32[128,2]{0,1:T(2,128)}, u32[]{:S(2)}) copy-start(s32[128,2]{0,1:T(2,128)} %param.10) | copy-start | bytes 3076
  106.8 8.6 %copy-start.1 = (bf16[512,768]{1,0:T(8,128)(2,1)S(1)}, bf16[512,768]{1,0:T(8,128)(2,1)}, u32[]{:S(2)}) copy-start(bf16[512,768]{1,0:T(8,128)(2,1)} %param.7) | copy-start | bytes 2359300
  106.8 246.8 %all-to-all-start = ((bf16[16,2,196608]{2,1,0:T(2,128)(2,1)}), bf16[16,2,196608]{2,1,0:T(2,128)(2,1)}, u32[]{:S(2)}, u32[]{:S(2)}) async-start(bf16[16,2,196608]{2,1,0:T(2,128)(2,1)} %stack.12), calls=%async_computation | async-start | bytes 25165824 | tf_op jit(solution)/shard_map/all_to_all | solution.py:46
  114.2 311.2 %all-gather.2.cloned.1.call-start = ((), (), s32[]{:S(2)}) async-start(), calls=%async_computation.5 | async-start | bytes 9437184 | tf_op jit(solution)/shard_map/all_gather | solution.py:73
  114.9 586.1 %reduce-scatter.2.cloned.1.call-start = ((), (), s32[]{:S(2)}) async-start(), calls=%async_computation.4 | async-start | bytes 9437184 | tf_op jit(solution)/shard_map/reduce_scatter | solution.py:69
  383.9 13.7 %copy-start = (bf16[8,64,6,128]{3,2,1,0:T(8,128)(2,1)S(1)}, bf16[8,64,6,128]{3,2,1,0:T(8,128)(2,1)}, u32[]{:S(2)}) copy-start(bf16[8,64,6,128]{3,2,1,0:T(8,128)(2,1)} %reshape.59) | copy-start | bytes 2359300
  555.2 117.2 %all-to-all-start.1 = ((bf16[16,2,98304]{2,1,0:T(2,128)(2,1)}), bf16[16,2,98304]{2,1,0:T(2,128)(2,1)}, u32[]{:S(2)}, u32[]{:S(2)}) async-start(bf16[16,2,98304]{2,1,0:T(2,128)(2,1)} %reshape.66), calls=%async_computation.2 | async-start | bytes 12582912 | tf_op jit(solution)/shard_map/all_to_all | solution.py:99
Sparse Core Ops, SparseCore 0:
  10.4 83.7 all-reduce.1
  116.7 50.5 all-gather.1
  425.5 49.5 reduce-scatter.1
